TPU v7x, 32 devices: a whole 2x2x4 slice. The times are simulated.
32 devices in a mesh: lat: 4 (over y, core), lon: 8 (over z, x).
Axes of the slice: x: 2, y: 2, z: 4, core: 2. Of those that a mesh axis runs over, the one named last changes fastest.
Arguments:
- field: bfloat16 [64, 128, 384], P('lat', 'lon'), may hold values from -6 to 6
- obs_jac: bfloat16 [32, 32, 128, 384], P(None, ('lat', 'lon')), may hold values from -0.3125 to 0.3125
- obs_frac: bfloat16 [32, 32, 2, 128], P(None, ('lat', 'lon')), may hold values from 0 to 1
- obs_innov: bfloat16 [32, 32, 128], P(None, ('lat', 'lon')), may hold values from -6 to 6
- obs_rinv: bfloat16 [32, 32, 128], P(None, ('lat', 'lon')), may hold values from 1 to 16
- obs_cells: int32 [32, 32, 128], P(None, ('lat', 'lon')), may hold values from -1 to 270, as said below
Outputs:
- departures: float32 [32, 32, 128], P(None, ('lat', 'lon'))
- field_grad: float32 [64, 128, 384], P('lat', 'lon')
Inputs may be any that keep to these rules, and one draw needn't show every extreme that they name: `obs_cells`: in block (o, p) the live slots come first, at least one and at most 128; a live slot holds r * 17 + q with r below 16 and q below 16; slot 0 of every block holds the cell at r = 15, q = 15; the number of live slots varies by owner.
All inputs are finite; a program needn't handle non-finite values.
Results may differ from a plain program's by a relative error of at most 0.0046.
Values may be sent and summed in bfloat16 or wider, within the bound.
A program may use at most 128 MiB of HBM per device.

v0:
```python
import jax
import jax.numpy as jnp
from jax import lax
from jax.sharding import PartitionSpec as P


def shifted(block, axis, distance):
    devices = range(lax.axis_size(axis))
    route = [(i - distance, i) for i in devices if i - distance in devices]
    return lax.ppermute(block, axis, route)


def passed_along(value, axis, steps):
    count = lax.axis_size(axis)
    pairs = [(source, (source + steps) % count) for source in range(count)]
    return lax.ppermute(value, axis, pairs)


def bilinear_weights(frac_lat, frac_lon):
    lat_part = frac_lat.astype(jnp.float32)
    lon_part = frac_lon.astype(jnp.float32)
    raw_weights = (
        (1.0 - lat_part) * (1.0 - lon_part),
        lat_part * (1.0 - lon_part),
        (1.0 - lat_part) * lon_part,
        lat_part * lon_part,
    )
    return lax.optimization_barrier(tuple((weight.astype(jnp.bfloat16) for weight in raw_weights)))


def spread_matrix(cell_ids, frac_lat, frac_lon, stride, cells_total):
    is_live = cell_ids >= 0
    corner = jnp.where(is_live, cell_ids, 0)
    weights = bilinear_weights(frac_lat, frac_lon)
    cell_axis = lax.broadcasted_iota(jnp.int32, (1, cells_total), 1)
    matrix = jnp.zeros((cell_ids.shape[0], cells_total), jnp.float32)
    for weight, offset in zip(weights, (0, stride, 1, stride + 1)):
        live_weight = jnp.where(is_live, weight.astype(jnp.float32), 0.0)
        matrix = matrix + jnp.where(
            corner[:, None] + offset == cell_axis, live_weight[:, None], 0.0
        )
    return matrix.astype(jnp.bfloat16)


def forward_piece(spread, col_table, cell_ids, innovation, jacobian):
    interp = jnp.dot(spread, col_table, preferred_element_type=jnp.float32)
    evolved = jnp.sum(interp * jacobian.astype(jnp.float32), axis=1)
    return jnp.where(
        cell_ids >= 0, evolved - innovation.astype(jnp.float32), jnp.zeros((), jnp.float32)
    )


def adjoint_piece(spread, inv_error, departure, jacobian, grad_ext):
    contrib = (
        (inv_error.astype(jnp.float32) * departure)[:, None] * jacobian.astype(jnp.float32)
    ).astype(jnp.bfloat16)
    return grad_ext + lax.dot_general(
        spread, contrib, (((0,), (0,)), ((), ())), preferred_element_type=jnp.float32
    )


def shards(field, obs_jac, obs_frac, obs_innov, obs_rinv, obs_cells):
    lat_rows, lon_cols, width_all = field.shape
    north_row = shifted(field[:1], "lat", -1)
    taller = jnp.concatenate([field, north_row], axis=0)
    east_col = passed_along(taller[:, :1], "lon", -1)
    widened = jnp.concatenate([taller, east_col], axis=1)
    stride = lon_cols + 1
    col_table = widened.reshape(-1, width_all)
    cells_total = col_table.shape[0]
    jac_rows, frac_pair, innov_vals, rinv_vals = (
        lax.all_to_all(obs_jac, ("lat", "lon"), split_axis=0, concat_axis=1, tiled=True),
        lax.all_to_all(obs_frac, ("lat", "lon"), split_axis=0, concat_axis=1, tiled=True),
        lax.all_to_all(obs_innov, ("lat", "lon"), split_axis=0, concat_axis=1, tiled=True),
        lax.all_to_all(obs_rinv, ("lat", "lon"), split_axis=0, concat_axis=1, tiled=True),
    )
    cell_vals = lax.all_to_all(obs_cells, ("lat", "lon"), split_axis=0, concat_axis=1, tiled=True)
    sources = cell_vals.shape[1]
    slots_all = cell_vals.shape[2]
    cells_two = cell_vals.reshape(sources, slots_all)
    frac_three = frac_pair.reshape(sources, 2, slots_all)
    innov_two = innov_vals.reshape(sources, slots_all)
    rinv_two = rinv_vals.reshape(sources, slots_all)
    jac_three = jac_rows.reshape(sources, slots_all, width_all)
    piece = slots_all // 8
    piece_rows = sources * piece

    def take_piece(piece_idx):
        start = piece_idx * piece
        cells_p = lax.dynamic_slice_in_dim(cells_two, start, piece, 1).reshape(-1)
        frac_p = lax.dynamic_slice_in_dim(frac_three, start, piece, 2)
        lat_p = frac_p[:, 0, :].reshape(-1)
        lon_p = frac_p[:, 1, :].reshape(-1)
        innov_p = lax.dynamic_slice_in_dim(innov_two, start, piece, 1).reshape(-1)
        rinv_p = lax.dynamic_slice_in_dim(rinv_two, start, piece, 1).reshape(-1)
        jac_p = lax.dynamic_slice_in_dim(jac_three, start, piece, 1).reshape(piece_rows, width_all)
        return (cells_p, lat_p, lon_p, innov_p, rinv_p, jac_p)

    def store_piece(departs, departure, piece_idx):
        return lax.dynamic_update_slice_in_dim(
            departs, departure.reshape(sources, piece), piece_idx * piece, 1
        )

    def full_turn(piece_idx, state_pair):
        grad_ext, departs = state_pair
        cells_p, lat_p, lon_p, innov_p, rinv_p, jac_p = take_piece(piece_idx)
        spread = spread_matrix(cells_p, lat_p, lon_p, stride, cells_total)
        departure = forward_piece(spread, col_table, cells_p, innov_p, jac_p)
        grad_ext = adjoint_piece(spread, rinv_p, departure, jac_p, grad_ext)
        return (grad_ext, store_piece(departs, departure, piece_idx))

    grad_start = jnp.zeros((cells_total, width_all), jnp.float32)
    depart_start = jnp.zeros((sources, slots_all), jnp.float32)
    live_most = jnp.max(jnp.sum((cells_two >= 0).astype(jnp.int32), axis=1))
    pieces_used = (live_most + piece - 1) // piece
    grad_ext, departs = lax.fori_loop(0, pieces_used, full_turn, (grad_start, depart_start))
    grad_grid = grad_ext.reshape(lat_rows + 1, stride, width_all)
    east_back = passed_along(grad_grid[:, lon_cols:], "lon", 1)
    grad_grid = grad_grid[:, :lon_cols].at[:, :1].add(east_back)
    north_back = shifted(grad_grid[lat_rows:], "lat", 1)
    field_grad = grad_grid[:lat_rows].at[:1].add(north_back)
    departures = lax.all_to_all(
        departs.reshape(1, sources, slots_all),
        ("lat", "lon"),
        split_axis=1,
        concat_axis=0,
        tiled=True,
    )
    return (departures, field_grad)


def solution(mesh):
    placed = (
        P("lat", "lon", None),
        P(None, ("lat", "lon"), None, None),
        P(None, ("lat", "lon"), None, None),
        P(None, ("lat", "lon"), None),
        P(None, ("lat", "lon"), None),
        P(None, ("lat", "lon"), None),
    )
    return jax.shard_map(
        shards,
        mesh=mesh,
        in_specs=placed,
        out_specs=(P(None, ("lat", "lon"), None), P("lat", "lon", None)),
        check_vma=False,
    )
```

profile of v0, /device:TPU:0, one launch (start us, length us, event | category | flops | bytes accessed | tf_op | source)
XLA Modules:
  0.0 184.6 jit_solution(12065559047575675687)
XLA Ops:
  0.6 1.3 copy.22
  1.9 7.3 %all-to-all-start.4 = ((bf16[32,1,128]{2,1,0:T(2,128)(2,1)}), bf16[32,1,128]{2,1,0:T(2,128)(2,1)S(1)}, u32[]{:S(2)}, u32[]{:S(2)}) async-start(bf16[32,1,128]{2,1,0:T(2,128)(2,1)} %copy.22), calls=%async_computation.4 | async-start | bytes 32768 | tf_op jit(solution)/shard_map/all_to_all | solution.py:74
  10.0 6.4 %all-to-all-done.4 = bf16[32,1,128]{2,1,0:T(2,128)(2,1)S(1)} async-done(((bf16[32,1,128]{2,1,0:T(2,128)(2,1)}), bf16[32,1,128]{2,1,0:T(2,128)(2,1)S(1)}, u32[]{:S(2)}, u32[]{:S(2)}) %all-to-all-start.4) | async-done | bytes 8224 | tf_op jit(solution)/shard_map/all_to_all | solution.py:74
  16.3 8.8 %all_to_all.27 = bf16[32,1,128]{2,1,0:T(2,128)(2,1)S(1)} all-to-all(bf16[32,1,128]{2,1,0:T(2,128)(2,1)S(1)} %copy.21), channel_id=1, replica_groups=mesh['lat'=4,'lon'=8] {'lat','lon'}, dimensions={0} | all-to-all | bytes 16384 | tf_op jit(solution)/shard_map/all_to_all | solution.py:75
  25.2 9.6 %all_to_all.28 = s32[32,1,128]{2,1,0:T(1,128)S(1)} all-to-all(s32[32,1,128]{2,1,0:T(1,128)} %param.17), channel_id=1, replica_groups=mesh['lat'=4,'lon'=8] {'lat','lon'}, dimensions={0} | all-to-all | bytes 32768 | tf_op jit(solution)/shard_map/all_to_all | solution.py:77
  34.8 9.6 %all_to_all.29 = bf16[32,1,2,128]{3,2,1,0:T(2,128)(2,1)S(1)} all-to-all(bf16[32,1,2,128]{3,2,1,0:T(2,128)(2,1)} %param.14), channel_id=1, replica_groups=mesh['lat'=4,'lon'=8] {'lat','lon'}, dimensions={0} | all-to-all | bytes 32768 | tf_op jit(solution)/shard_map/all_to_all | solution.py:73
  44.4 3.7 %all-to-all-start.3 = ((bf16[32,1,128,384]{3,2,1,0:T(8,128)(2,1)}), bf16[32,1,128,384]{3,2,1,0:T(8,128)(2,1)}, u32[]{:S(2)}, u32[]{:S(2)}) async-start(bf16[32,1,128,384]{3,2,1,0:T(8,128)(2,1)} %param.13), calls=%async_computation.3 | async-start | bytes 6291456 | tf_op jit(solution)/shard_map/all_to_all | solution.py:72
  48.1 1.3 collective-permute-start
  49.4 1.7 collective-permute-done
  51.2 4.5 %collective-permute-start.1 = (bf16[17,1,384]{2,1,0:T(2,128)(2,1)S(1)}, bf16[17,1,384]{2,1,0:T(2,128)(2,1)S(1)}, u32[]{:S(2)}, u32[]{:S(2)}) collective-permute-start(bf16[17,1,384]{2,1,0:T(2,128)(2,1)S(1)} %slice.82), channel_id=1, source_target_pairs={{0,7},{1,0},{2,1},{3,2},{4,3},{5,4},{6,5},{7,6},{8,15},{9,8},{10,9... | collective-permute-start | bytes 39176 | tf_op jit(solution)/shard_map/ppermute | solution.py:16
  55.7 44.9 %collective-permute-done.1 = bf16[17,1,384]{2,1,0:T(2,128)(2,1)S(1)} collective-permute-done((bf16[17,1,384]{2,1,0:T(2,128)(2,1)S(1)}, bf16[17,1,384]{2,1,0:T(2,128)(2,1)S(1)}, u32[]{:S(2)}, u32[]{:S(2)}) %collective-permute-start.1) | collective-permute-done | bytes 13088 | tf_op jit(solution)/shard_map/ppermute | solution.py:16
  102.2 18.4 %all-to-all-done.3 = bf16[32,1,128,384]{3,2,1,0:T(8,128)(2,1)} async-done(((bf16[32,1,128,384]{3,2,1,0:T(8,128)(2,1)}), bf16[32,1,128,384]{3,2,1,0:T(8,128)(2,1)}, u32[]{:S(2)}, u32[]{:S(2)}) %all-to-all-start.3) | async-done | bytes 3145760 | tf_op jit(solution)/shard_map/all_to_all | solution.py:72
  121.2 12.5 %while.14 = (s32[]{:T(128)}, f32[289,384]{1,0:T(8,128)S(1)}, f32[32,128]{1,0:T(8,128)}, s32[]{:T(128)}, s32[32,128]{1,0:T(8,128)S(1)}, /*index=5*/bf16[32,2,128]...) while((s32[]{:T(128)}, f32[289,384]{1,0:T(8,128)S(1)}, ...), condition=%wide.region_4.5_spmd, body=%wide.region_2.4_spmd.sunk | while | flops 231940992 | bytes 6360035 | solution.py:116
  121.7 1.1 constant_dynamic-slice_fusion.7
  123.2 1.4 fusion.9
  124.8 1.1 convolution_add_fusion.2
  126.1 1.3 dynamic_update_slice.4
  129.4 1.4 fusion.9
  131.1 1.1 convolution_add_fusion.2
  132.3 1.4 dynamic_update_slice.4
  133.8 37.5 %collective-permute-start.2 = (f32[17,1,384]{2,1,0:T(1,128)S(1)}, f32[17,1,384]{2,1,0:T(1,128)S(1)}, u32[]{:S(2)}, u32[]{:S(2)}) collective-permute-start(f32[17,1,384]{2,1,0:T(1,128)S(1)} %slice.85), channel_id=1, source_target_pairs={{0,1},{1,2},{2,3},{3,4},{4,5},{5,6},{6,7},{7,0},{8,9},{9,10},{10,1... | collective-permute-start | bytes 78344 | tf_op jit(solution)/shard_map/ppermute | solution.py:16
  171.4 5.3 %all-to-all-start.5 = ((f32[1,32,128]{2,0,1:T(1,128)}), f32[1,32,128]{2,0,1:T(1,128)S(1)}, u32[]{:S(2)}, u32[]{:S(2)}) async-start(f32[1,32,128]{2,0,1:T(1,128)} %bitcast.4), calls=%async_computation.5 | async-start | bytes 32768 | tf_op jit(solution)/shard_map/all_to_all | solution.py:122
  176.9 2.2 %collective-permute-start.3 = (f32[1,16,384]{2,1,0:T(8,128)S(1)}, f32[1,16,384]{2,1,0:T(8,128)S(1)}, u32[]{:S(2)}, u32[]{:S(2)}) collective-permute-start(f32[1,16,384]{2,1,0:T(8,128)S(1)} %slice.88), channel_id=1, source_target_pairs={{0,8},{8,16},{16,24},{1,9},{9,17},{17,25},{2,10},{10,18},{18,26},{... | collective-permute-start | bytes 73736 | tf_op jit(solution)/shard_map/ppermute | solution.py:10
  179.1 4.7 %all-to-all-done.5 = f32[1,32,128]{2,0,1:T(1,128)S(1)} async-done(((f32[1,32,128]{2,0,1:T(1,128)}), f32[1,32,128]{2,0,1:T(1,128)S(1)}, u32[]{:S(2)}, u32[]{:S(2)}) %all-to-all-start.5) | async-done | bytes 16416 | tf_op jit(solution)/shard_map/all_to_all | solution.py:122
  (67 shorter events, 6.8 us)
Async XLA Ops:
  1.9 14.4 %all-to-all-start.4 = ((bf16[32,1,128]{2,1,0:T(2,128)(2,1)}), bf16[32,1,128]{2,1,0:T(2,128)(2,1)S(1)}, u32[]{:S(2)}, u32[]{:S(2)}) async-start(bf16[32,1,128]{2,1,0:T(2,128)(2,1)} %copy.22), calls=%async_computation.4 | async-start | bytes 32768 | tf_op jit(solution)/shard_map/all_to_all | solution.py:74
  44.4 3.7 %copy-start.1 = (bf16[16,16,384]{2,1,0:T(8,128)(2,1)S(1)}, bf16[16,16,384]{2,1,0:T(8,128)(2,1)}, u32[]{:S(2)}) copy-start(bf16[16,16,384]{2,1,0:T(8,128)(2,1)} %param.12) | copy-start | bytes 589828
  44.4 76.2 %all-to-all-start.3 = ((bf16[32,1,128,384]{3,2,1,0:T(8,128)(2,1)}), bf16[32,1,128,384]{3,2,1,0:T(8,128)(2,1)}, u32[]{:S(2)}, u32[]{:S(2)}) async-start(bf16[32,1,128,384]{3,2,1,0:T(8,128)(2,1)} %param.13), calls=%async_computation.3 | async-start | bytes 6291456 | tf_op jit(solution)/shard_map/all_to_all | solution.py:72
  48.1 3.1 %collective-permute-start = (bf16[1,16,384]{2,1,0:T(8,128)(2,1)S(1)}, bf16[1,16,384]{2,1,0:T(8,128)(2,1)S(1)}, u32[]{:S(2)}, u32[]{:S(2)}) collective-permute-start(bf16[1,16,384]{2,1,0:T(8,128)(2,1)S(1)} %slice.74), channel_id=1, source_target_pairs={{8,0},{16,8},{24,16},{9,1},{17,9},{25,17},{10,2},{18,10},{26,18},{... | collective-permute-start | bytes 36872 | tf_op jit(solution)/shard_map/ppermute | solution.py:10
  51.2 49.5 %collective-permute-start.1 = (bf16[17,1,384]{2,1,0:T(2,128)(2,1)S(1)}, bf16[17,1,384]{2,1,0:T(2,128)(2,1)S(1)}, u32[]{:S(2)}, u32[]{:S(2)}) collective-permute-start(bf16[17,1,384]{2,1,0:T(2,128)(2,1)S(1)} %slice.82), channel_id=1, source_target_pairs={{0,7},{1,0},{2,1},{3,2},{4,3},{5,4},{6,5},{7,6},{8,15},{9,8},{10,9... | collective-permute-start | bytes 39176 | tf_op jit(solution)/shard_map/ppermute | solution.py:16
  133.8 42.9 %collective-permute-start.2 = (f32[17,1,384]{2,1,0:T(1,128)S(1)}, f32[17,1,384]{2,1,0:T(1,128)S(1)}, u32[]{:S(2)}, u32[]{:S(2)}) collective-permute-start(f32[17,1,384]{2,1,0:T(1,128)S(1)} %slice.85), channel_id=1, source_target_pairs={{0,1},{1,2},{2,3},{3,4},{4,5},{5,6},{6,7},{7,0},{8,9},{9,10},{10,1... | collective-permute-start | bytes 78344 | tf_op jit(solution)/shard_map/ppermute | solution.py:16
  171.4 12.4 %all-to-all-start.5 = ((f32[1,32,128]{2,0,1:T(1,128)}), f32[1,32,128]{2,0,1:T(1,128)S(1)}, u32[]{:S(2)}, u32[]{:S(2)}) async-start(f32[1,32,128]{2,0,1:T(1,128)} %bitcast.4), calls=%async_computation.5 | async-start | bytes 32768 | tf_op jit(solution)/shard_map/all_to_all | solution.py:122
  176.9 6.9 %collective-permute-start.3 = (f32[1,16,384]{2,1,0:T(8,128)S(1)}, f32[1,16,384]{2,1,0:T(8,128)S(1)}, u32[]{:S(2)}, u32[]{:S(2)}) collective-permute-start(f32[1,16,384]{2,1,0:T(8,128)S(1)} %slice.88), channel_id=1, source_target_pairs={{0,8},{8,16},{16,24},{1,9},{9,17},{17,25},{2,10},{10,18},{18,26},{... | collective-permute-start | bytes 73736 | tf_op jit(solution)/shard_map/ppermute | solution.py:10
  183.8 0.8 copy-start
where the time goes:
time: 186 us; the launch traced here: 185 us
  waiting for transfers between devices  76.1 us (41%)
  starting transfers between devices  61.8 us (33%)
  blocking collectives  28 us (15%)
  local copies, waits for them, and re-layouts  10.5 us (6%)
  matrix products  5.04 us (3%)
    ppermute x2, waiting for transfers between devices, passed_along(): return lax.ppermute(value, axis, pairs)  44.9 us
    ppermute x2, starting transfers between devices, passed_along(): return lax.ppermute(value, axis, pairs)  42.1 us
    all_to_all x1, waiting for transfers between devices, shards(): lax.all_to_all(obs_jac, ('lat', 'lon'), split_axis=0, concat_axis=1, tile...  18.4 us
    all_to_all x1, blocking collectives, shards(): lax.all_to_all(obs_cells, ('lat', 'lon'), split_axis=0, concat_axis=1, ti...  9.61 us
    all_to_all x1, blocking collectives, shards(): lax.all_to_all(obs_frac, ('lat', 'lon'), split_axis=0, concat_axis=1, til...  9.61 us
    all_to_all x1, blocking collectives, shards(): lax.all_to_all(obs_rinv, ('lat', 'lon'), split_axis=0, concat_axis=1, til...  8.82 us
    all_to_all x1, starting transfers between devices, shards(): lax.all_to_all(obs_innov, ('lat', 'lon'), split_axis=0, concat_axis=1, ti...  7.33 us
    all_to_all x1, waiting for transfers between devices, shards(): lax.all_to_all(obs_innov, ('lat', 'lon'), split_axis=0, concat_axis=1, ti...  6.35 us
  transfers between devices with their start and end apart: 7, of which 5 were waited for; matrix products, arithmetic and copies ran while one was open for 1% of the time, Pallas kernels for 0%

commit v1 on v0

--- a/solution.py
+++ b/solution.py
@@ -68,10 +68,19 @@
     stride = lon_cols + 1
     col_table = widened.reshape(-1, width_all)
     cells_total = col_table.shape[0]
+    apply_the_shifts_all = lambda mat: jnp.concatenate(
+        lax.all_to_all(
+            jnp.stack(jnp.split(mat, lax.axis_size(("lat", "lon")), 0), 0),
+            axis_name=("lat", "lon"),
+            split_axis=0,
+            concat_axis=0,
+        ),
+        1,
+    )
     jac_rows, frac_pair, innov_vals, rinv_vals = (
         lax.all_to_all(obs_jac, ("lat", "lon"), split_axis=0, concat_axis=1, tiled=True),
         lax.all_to_all(obs_frac, ("lat", "lon"), split_axis=0, concat_axis=1, tiled=True),
-        lax.all_to_all(obs_innov, ("lat", "lon"), split_axis=0, concat_axis=1, tiled=True),
+        apply_the_shifts_all(obs_innov),
         lax.all_to_all(obs_rinv, ("lat", "lon"), split_axis=0, concat_axis=1, tiled=True),
     )
     cell_vals = lax.all_to_all(obs_cells, ("lat", "lon"), split_axis=0, concat_axis=1, tiled=True)

time: 186 us -> 224 us (1.20)
  local copies, waits for them, and re-layouts: 10.5 us -> 47.4 us
    unnamed x10 -> x40, local copies, waits for them, and re-layouts: 2.81 us -> 38.5 us
where the time goes in v1:
time: 224 us; the launch traced here: 221 us
  waiting for transfers between devices  76.1 us (34%)
  starting transfers between devices  61.8 us (28%)
  local copies, waits for them, and re-layouts  47.4 us (21%)
  blocking collectives  28 us (12%)
  matrix products  5.04 us (2%)
    ppermute x2, waiting for transfers between devices, passed_along(): return lax.ppermute(value, axis, pairs)  44.9 us
    ppermute x2, starting transfers between devices, passed_along(): return lax.ppermute(value, axis, pairs)  42.1 us
    unnamed x40, local copies, waits for them, and re-layouts  38.5 us
    all_to_all x1, waiting for transfers between devices, shards(): lax.all_to_all(obs_jac, ('lat', 'lon'), split_axis=0, concat_axis=1, tile...  18.4 us
    all_to_all x1, blocking collectives, shards(): lax.all_to_all(obs_cells, ('lat', 'lon'), split_axis=0, concat_axis=1, ti...  9.61 us
    all_to_all x1, blocking collectives, shards(): lax.all_to_all(obs_frac, ('lat', 'lon'), split_axis=0, concat_axis=1, til...  9.61 us
    all_to_all x1, blocking collectives, shards(): lax.all_to_all(obs_rinv, ('lat', 'lon'), split_axis=0, concat_axis=1, til...  8.82 us
    all_to_all x1, starting transfers between devices, shards(): lax.all_to_all(jnp.stack(jnp.split(mat, lax.axis_size(('lat', 'lon')), 0)...  7.33 us
  transfers between devices with their start and end apart: 7, of which 5 were waited for; matrix products, arithmetic and copies ran while one was open for 1% of the time, Pallas kernels for 0%

profile of v1, /device:TPU:0, one launch (start us, length us, event | category | flops | bytes accessed | tf_op | source)
XLA Modules:
  0.0 221.5 jit_solution(17571124371428709415)
XLA Ops:
  1.8 1.2 constant_dynamic-update-slice_fusion.32
  5.4 1.2 constant_dynamic-update-slice_fusion.29
  7.8 1.2 constant_dynamic-update-slice_fusion.27
  18.6 1.2 constant_dynamic-update-slice_fusion.18
  38.9 7.3 %all-to-all-start.4 = ((bf16[32,1,1,128]{3,2,1,0:T(2,128)(2,1)}), bf16[32,1,1,128]{3,2,1,0:T(2,128)(2,1)S(1)}, u32[]{:S(2)}, u32[]{:S(2)}) async-start(bf16[32,1,1,128]{3,2,1,0:T(2,128)(2,1)} %constant_dynamic-update-slice_fusion.2), calls=%async_computation.4 | async-start | bytes 32768 | tf_op jit(solution)/shard_map/all_to_all | solution.py:72
  46.9 6.4 %all-to-all-done.4 = bf16[32,1,1,128]{3,2,1,0:T(2,128)(2,1)S(1)} async-done(((bf16[32,1,1,128]{3,2,1,0:T(2,128)(2,1)}), bf16[32,1,1,128]{3,2,1,0:T(2,128)(2,1)S(1)}, u32[]{:S(2)}, u32[]{:S(2)}) %all-to-all-start.4) | async-done | bytes 8224 | tf_op jit(solution)/shard_map/all_to_all | solution.py:72
  53.3 8.8 %all_to_all.53 = bf16[32,1,128]{2,1,0:T(2,128)(2,1)S(1)} all-to-all(bf16[32,1,128]{2,1,0:T(2,128)(2,1)S(1)} %copy.20), channel_id=1, replica_groups=mesh['lat'=4,'lon'=8] {'lat','lon'}, dimensions={0} | all-to-all | bytes 16384 | tf_op jit(solution)/shard_map/all_to_all | solution.py:84
  62.1 9.6 %all_to_all.54 = s32[32,1,128]{2,1,0:T(1,128)S(1)} all-to-all(s32[32,1,128]{2,1,0:T(1,128)} %param.17), channel_id=1, replica_groups=mesh['lat'=4,'lon'=8] {'lat','lon'}, dimensions={0} | all-to-all | bytes 32768 | tf_op jit(solution)/shard_map/all_to_all | solution.py:86
  71.7 9.6 %all_to_all.55 = bf16[32,1,2,128]{3,2,1,0:T(2,128)(2,1)S(1)} all-to-all(bf16[32,1,2,128]{3,2,1,0:T(2,128)(2,1)} %param.14), channel_id=1, replica_groups=mesh['lat'=4,'lon'=8] {'lat','lon'}, dimensions={0} | all-to-all | bytes 32768 | tf_op jit(solution)/shard_map/all_to_all | solution.py:82
  81.3 3.7 %all-to-all-start.3 = ((bf16[32,1,128,384]{3,2,1,0:T(8,128)(2,1)}), bf16[32,1,128,384]{3,2,1,0:T(8,128)(2,1)}, u32[]{:S(2)}, u32[]{:S(2)}) async-start(bf16[32,1,128,384]{3,2,1,0:T(8,128)(2,1)} %param.13), calls=%async_computation.3 | async-start | bytes 6291456 | tf_op jit(solution)/shard_map/all_to_all | solution.py:81
  85.0 1.3 collective-permute-start
  86.3 1.7 collective-permute-done
  88.1 4.5 %collective-permute-start.1 = (bf16[17,1,384]{2,1,0:T(2,128)(2,1)S(1)}, bf16[17,1,384]{2,1,0:T(2,128)(2,1)S(1)}, u32[]{:S(2)}, u32[]{:S(2)}) collective-permute-start(bf16[17,1,384]{2,1,0:T(2,128)(2,1)S(1)} %slice.82), channel_id=1, source_target_pairs={{0,7},{1,0},{2,1},{3,2},{4,3},{5,4},{6,5},{7,6},{8,15},{9,8},{10,9... | collective-permute-start | bytes 39176 | tf_op jit(solution)/shard_map/ppermute | solution.py:16
  92.7 44.9 %collective-permute-done.1 = bf16[17,1,384]{2,1,0:T(2,128)(2,1)S(1)} collective-permute-done((bf16[17,1,384]{2,1,0:T(2,128)(2,1)S(1)}, bf16[17,1,384]{2,1,0:T(2,128)(2,1)S(1)}, u32[]{:S(2)}, u32[]{:S(2)}) %collective-permute-start.1) | collective-permute-done | bytes 13088 | tf_op jit(solution)/shard_map/ppermute | solution.py:16
  139.2 18.4 %all-to-all-done.3 = bf16[32,1,128,384]{3,2,1,0:T(8,128)(2,1)} async-done(((bf16[32,1,128,384]{3,2,1,0:T(8,128)(2,1)}), bf16[32,1,128,384]{3,2,1,0:T(8,128)(2,1)}, u32[]{:S(2)}, u32[]{:S(2)}) %all-to-all-start.3) | async-done | bytes 3145760 | tf_op jit(solution)/shard_map/all_to_all | solution.py:81
  158.2 12.5 %while.14 = (s32[]{:T(128)}, f32[289,384]{1,0:T(8,128)S(1)}, f32[32,128]{1,0:T(8,128)}, s32[]{:T(128)}, s32[32,128]{1,0:T(8,128)S(1)}, /*index=5*/bf16[32,2,128]...) while((s32[]{:T(128)}, f32[289,384]{1,0:T(8,128)S(1)}, ...), condition=%wide.region_4.5_spmd, body=%wide.region_2.4_spmd.sunk | while | flops 231940992 | bytes 6360035 | solution.py:125
  160.1 1.4 fusion.9
  163.0 1.3 dynamic_update_slice.4
  166.3 1.4 fusion.9
  169.3 1.4 dynamic_update_slice.4
  170.8 37.5 %collective-permute-start.2 = (f32[17,1,384]{2,1,0:T(1,128)S(1)}, f32[17,1,384]{2,1,0:T(1,128)S(1)}, u32[]{:S(2)}, u32[]{:S(2)}) collective-permute-start(f32[17,1,384]{2,1,0:T(1,128)S(1)} %slice.85), channel_id=1, source_target_pairs={{0,1},{1,2},{2,3},{3,4},{4,5},{5,6},{6,7},{7,0},{8,9},{9,10},{10,1... | collective-permute-start | bytes 78344 | tf_op jit(solution)/shard_map/ppermute | solution.py:16
  208.3 5.3 %all-to-all-start.5 = ((f32[1,32,128]{2,0,1:T(1,128)}), f32[1,32,128]{2,0,1:T(1,128)S(1)}, u32[]{:S(2)}, u32[]{:S(2)}) async-start(f32[1,32,128]{2,0,1:T(1,128)} %bitcast.36), calls=%async_computation.5 | async-start | bytes 32768 | tf_op jit(solution)/shard_map/all_to_all | solution.py:131
  213.8 2.2 collective-permute-start.3
  216.0 4.7 %all-to-all-done.5 = f32[1,32,128]{2,0,1:T(1,128)S(1)} async-done(((f32[1,32,128]{2,0,1:T(1,128)}), f32[1,32,128]{2,0,1:T(1,128)S(1)}, u32[]{:S(2)}, u32[]{:S(2)}) %all-to-all-start.5) | async-done | bytes 16416 | tf_op jit(solution)/shard_map/all_to_all | solution.py:131
  (98 shorter events, 43.5 us)
Async XLA Ops:
  38.9 14.4 %all-to-all-start.4 = ((bf16[32,1,1,128]{3,2,1,0:T(2,128)(2,1)}), bf16[32,1,1,128]{3,2,1,0:T(2,128)(2,1)S(1)}, u32[]{:S(2)}, u32[]{:S(2)}) async-start(bf16[32,1,1,128]{3,2,1,0:T(2,128)(2,1)} %constant_dynamic-update-slice_fusion.2), calls=%async_computation.4 | async-start | bytes 32768 | tf_op jit(solution)/shard_map/all_to_all | solution.py:72
  81.3 3.7 %copy-start.1 = (bf16[16,16,384]{2,1,0:T(8,128)(2,1)S(1)}, bf16[16,16,384]{2,1,0:T(8,128)(2,1)}, u32[]{:S(2)}) copy-start(bf16[16,16,384]{2,1,0:T(8,128)(2,1)} %param.12) | copy-start | bytes 589828
  81.3 76.2 %all-to-all-start.3 = ((bf16[32,1,128,384]{3,2,1,0:T(8,128)(2,1)}), bf16[32,1,128,384]{3,2,1,0:T(8,128)(2,1)}, u32[]{:S(2)}, u32[]{:S(2)}) async-start(bf16[32,1,128,384]{3,2,1,0:T(8,128)(2,1)} %param.13), calls=%async_computation.3 | async-start | bytes 6291456 | tf_op jit(solution)/shard_map/all_to_all | solution.py:81
  85.0 3.1 %collective-permute-start = (bf16[1,16,384]{2,1,0:T(8,128)(2,1)S(1)}, bf16[1,16,384]{2,1,0:T(8,128)(2,1)S(1)}, u32[]{:S(2)}, u32[]{:S(2)}) collective-permute-start(bf16[1,16,384]{2,1,0:T(8,128)(2,1)S(1)} %slice.74), channel_id=1, source_target_pairs={{8,0},{16,8},{24,16},{9,1},{17,9},{25,17},{10,2},{18,10},{26,18},{... | collective-permute-start | bytes 36872 | tf_op jit(solution)/shard_map/ppermute | solution.py:10
  88.1 49.5 %collective-permute-start.1 = (bf16[17,1,384]{2,1,0:T(2,128)(2,1)S(1)}, bf16[17,1,384]{2,1,0:T(2,128)(2,1)S(1)}, u32[]{:S(2)}, u32[]{:S(2)}) collective-permute-start(bf16[17,1,384]{2,1,0:T(2,128)(2,1)S(1)} %slice.82), channel_id=1, source_target_pairs={{0,7},{1,0},{2,1},{3,2},{4,3},{5,4},{6,5},{7,6},{8,15},{9,8},{10,9... | collective-permute-start | bytes 39176 | tf_op jit(solution)/shard_map/ppermute | solution.py:16
  170.8 42.9 %collective-permute-start.2 = (f32[17,1,384]{2,1,0:T(1,128)S(1)}, f32[17,1,384]{2,1,0:T(1,128)S(1)}, u32[]{:S(2)}, u32[]{:S(2)}) collective-permute-start(f32[17,1,384]{2,1,0:T(1,128)S(1)} %slice.85), channel_id=1, source_target_pairs={{0,1},{1,2},{2,3},{3,4},{4,5},{5,6},{6,7},{7,0},{8,9},{9,10},{10,1... | collective-permute-start | bytes 78344 | tf_op jit(solution)/shard_map/ppermute | solution.py:16
  208.3 12.4 %all-to-all-start.5 = ((f32[1,32,128]{2,0,1:T(1,128)}), f32[1,32,128]{2,0,1:T(1,128)S(1)}, u32[]{:S(2)}, u32[]{:S(2)}) async-start(f32[1,32,128]{2,0,1:T(1,128)} %bitcast.36), calls=%async_computation.5 | async-start | bytes 32768 | tf_op jit(solution)/shard_map/all_to_all | solution.py:131
  213.8 6.9 %collective-permute-start.3 = (f32[1,16,384]{2,1,0:T(8,128)S(1)}, f32[1,16,384]{2,1,0:T(8,128)S(1)}, u32[]{:S(2)}, u32[]{:S(2)}) collective-permute-start(f32[1,16,384]{2,1,0:T(8,128)S(1)} %slice.88), channel_id=1, source_target_pairs={{0,8},{8,16},{16,24},{1,9},{9,17},{17,25},{2,10},{10,18},{18,26},{... | collective-permute-start | bytes 73736 | tf_op jit(solution)/shard_map/ppermute | solution.py:10
  220.7 0.8 copy-start
